TPU v7x, 32 devices: a whole 2x2x4 slice. The times are simulated.
32 devices in a mesh: facet: 8 (over y, x, core), sub: 4 (over z).
Axes of the slice: x: 2, y: 2, z: 4, core: 2. Of those that a mesh axis runs over, the one named last changes fastest.
Arguments:
- facet_spec: bfloat16 [8, 2, 704, 448], P('facet'), may hold values from -3 to 3
- worker_of_subgrid: int32 [32], replicated, may hold values from 0 to 31, each once
- vis_count: int32 [32], P(('facet', 'sub')), may hold values from 512 to 8192, as said below
- bin_offsets: int32 [32, 2, 8192], P(('facet', 'sub')), may hold values from 0 to 248
- bin_fractions: float32 [32, 2, 8192], P(('facet', 'sub')), may hold values from 0 to 1
- observed: float32 [32, 2, 8192], P(('facet', 'sub')), may hold values from -6 to 6
Outputs:
- residual_vis: float32 [32, 2, 8192], P(('facet', 'sub'))
- facet_update: float32 [8, 2, 704, 448], P('facet', None, 'sub')
Inputs may be any that keep to these rules, and one draw needn't show every extreme that they name: `worker_of_subgrid`: a permutation of the subgrids. `vis_count`: some device row has all 8192 slots live in every draw.
All inputs are finite; a program needn't handle non-finite values.
Results may differ from a plain program's by a relative error of at most 0.014.
Values may be sent and summed in bfloat16 or wider, within the bound.
A program may use at most 128 MiB of HBM per device.

v0:
```python
import functools
import math

import jax
import jax.numpy as jnp
import numpy as np
from jax import lax
from jax.experimental import pallas as pl
from jax.experimental.pallas import tpu as pltpu
from jax.sharding import PartitionSpec as P

SUB = 256
MC = 256
STEP = 64
KS = 8
VB = 512
MESH = pl.DeviceIdType.MESH
VMEM = pl.BlockSpec(memory_space=pltpu.VMEM)
SMEM = pl.BlockSpec(memory_space=pltpu.SMEM)
F32 = jnp.float32
BF16 = jnp.bfloat16


def flip(index, bit):
    return index + bit - 2 * bit * ((index // bit) % 2)


def bits_of(count):
    return [1 << level for level in range(count.bit_length() - 1)]


def routes(count):
    bits = bits_of(count)
    return (bits, bits[:1] + bits[:0:-1])


def greet(count):
    me = lax.axis_index("facet")
    barrier = pltpu.get_barrier_semaphore()
    bits = bits_of(count)
    for bit in bits:
        pl.semaphore_signal(
            barrier, inc=1, device_id={"facet": flip(me, bit)}, device_id_type=MESH
        )
    pl.semaphore_wait(barrier, len(bits))


def remote(src, dst, send, recv, axis, target):
    return pltpu.make_async_remote_copy(
        src_ref=src,
        dst_ref=dst,
        send_sem=send,
        recv_sem=recv,
        device_id={axis: target},
        device_id_type=MESH,
    )


def transform_kernel(
    facets, pos_v, base, turns, worker, spec, slabs, left_adjoint, right_table,
    turned_table, corners, left_table, holder
):
    cols = spec.shape[3]
    pad = (pos_v - 1) * STEP
    me = lax.axis_index("facet")
    rank = lax.axis_index("sub")

    def note(subgrid, carry):
        holder[worker[subgrid]] = subgrid
        return carry

    lax.fori_loop(0, worker.shape[0], note, 0)
    for slab in range(facets):
        member = me
        for bit in bits_of(facets):
            member = flip(member, bit) if slab & bit else member
        subgrid = holder[member * pos_v + rank]
        corners[0, slab] = subgrid // pos_v * STEP
        corners[1, slab] = pad - subgrid % pos_v * STEP

    def turned(facet):
        turn = turns[facet]
        real, imag = turn[0:1], turn[1:2]
        return (base[0] * real - base[1] * imag, base[0] * imag + base[1] * real)

    real, imag = turned(me)
    left_adjoint[:MC, :SUB] = real.astype(BF16)
    left_adjoint[:MC, SUB:] = imag.astype(BF16)
    left_adjoint[MC:, :SUB] = (-imag).astype(BF16)
    left_adjoint[MC:, SUB:] = real.astype(BF16)
    real, imag = real.T, imag.T
    left_table[:SUB, :MC] = real.astype(BF16)
    left_table[:SUB, MC:] = (-imag).astype(BF16)
    left_table[SUB:, :MC] = imag.astype(BF16)
    left_table[SUB:, MC:] = real.astype(BF16)
    real, imag = turned((5 * me + 3) % facets)
    for table, first, second in ((right_table, real, imag), (turned_table, -imag, real)):
        table[:pad] = jnp.zeros((pad, 2 * SUB), BF16)
        table[pad + MC :] = jnp.zeros((pad, 2 * SUB), BF16)
        table[pad : pad + MC, :SUB] = first.astype(BF16)
        table[pad : pad + MC, SUB:] = second.astype(BF16)

    def transform(slab, carry):
        top = pl.multiple_of(corners[0, slab], STEP)
        left = pl.multiple_of(corners[1, slab], STEP)
        window = jnp.concatenate(
            [spec[0, 0, pl.ds(top, MC), :], spec[0, 1, pl.ds(top, MC), :]], axis=0
        )
        table = right_table[pl.ds(left, cols), :]
        mixed = jnp.dot(window, table, preferred_element_type=F32)
        real = mixed[:MC, :SUB] - mixed[MC:, SUB:]
        imag = mixed[:MC, SUB:] + mixed[MC:, :SUB]
        half = jnp.concatenate([real, imag], axis=0).astype(BF16)
        value = jnp.dot(left_table[...], half, preferred_element_type=F32)
        slabs[slab] = value.astype(BF16).reshape(2, SUB, SUB)
        return carry

    lax.fori_loop(0, facets, transform, 0, unroll=2)


def halve_kernel(facets, slabs, grid_out, total, landed, send, recv):
    me = lax.axis_index("facet")
    greet(facets)
    orders = routes(facets)
    levels = len(orders[0])
    sent = []

    def queue(part, level, held):
        rank = lambda slab: tuple(not slab & bit for bit in orders[part][level:])
        return sorted(held, key=rank)

    def copy_of(source, level, slab, part):
        bit = orders[part][level]
        return remote(
            source.at[slab, part], landed.at[level, slab - bit, part],
            send.at[2 * level + part, slab], recv.at[2 * level + part, slab - bit],
            "facet", flip(me, bit),
        )

    def post(source, level, slab, part):
        copy = copy_of(source, level, slab, part)
        copy.start()
        sent.append(copy)

    held = [list(range(facets))] * 2
    pairs = [queue(part, 0, [s for s in held[part] if s & 1]) for part in range(2)]
    for both in zip(*pairs):
        for part, slab in enumerate(both):
            post(slabs, 0, slab, part)
    for level in range(levels):
        held = [[s for s in held[p] if not s & orders[p][level]] for p in range(2)]
        pairs = [queue(part, level + 1, held[part]) for part in range(2)]
        for both in zip(*pairs):
            for part, slab in enumerate(both):
                copy_of(slabs, level, slab + orders[part][level], part).wait_recv()
                source = slabs if level == 0 else total
                value = source[slab, part].astype(F32) + landed[level, slab, part].astype(F32)
                if level == levels - 1:
                    grid_out[part] = value.astype(BF16)
                else:
                    total[slab, part] = value.astype(BF16)
                    if slab & orders[part][level + 1]:
                        post(total, level + 1, slab, part)
    for copy in sent:
        copy.wait_send()


def kernel_columns(offsets, fractions):
    cells = lax.broadcasted_iota(jnp.int32, (SUB, offsets.shape[1]), 0).astype(F32)
    scale = math.sqrt(math.log2(math.e)) * 9.0 / KS
    centred = cells - (offsets.astype(F32) + (0.5 * KS - 0.5))
    distance = centred * scale - (fractions - 0.5) * scale
    inside = jnp.abs(centred) < 0.5 * KS
    return jnp.where(inside, jnp.exp2(-1.0 - distance * distance), 0.0).astype(BF16)


def vis_kernel(count, grid, offsets, fractions, observed, residual, gridded, flipped, total):
    slots = offsets.shape[2]
    live_count = count[0]
    flipped[:SUB] = grid[0].astype(F32).T.astype(BF16)
    flipped[SUB:] = grid[1].astype(F32).T.astype(BF16)
    total[...] = jnp.zeros_like(total)
    residual[...] = jnp.zeros_like(residual)

    def half_block(first):
        span = pl.ds(first, VB)
        u_weights = kernel_columns(offsets[0, 0:1, span], fractions[0, 0:1, span])
        v_weights = kernel_columns(offsets[0, 1:2, span], fractions[0, 1:2, span])
        v_float = v_weights.astype(F32)
        product = jnp.dot(flipped[...], u_weights, preferred_element_type=F32)
        live = first + lax.broadcasted_iota(jnp.int32, (1, VB), 1) < live_count
        weighted = []
        for part in range(2):
            model = jnp.sum(product[part * SUB : (part + 1) * SUB] * v_float, axis=0, keepdims=True)
            row = jnp.where(live, observed[0, part : part + 1, span] - model, 0.0)
            residual[0, part : part + 1, span] = row
            weighted.append((row * v_float).astype(BF16))
        return lax.dot_general(
            u_weights,
            jnp.concatenate(weighted, axis=0),
            (((1,), (1,)), ((), ())),
            preferred_element_type=F32,
        )

    def block(index, carry):
        first = pl.multiple_of(index * 2 * VB, 2 * VB)
        total[...] += half_block(first) + half_block(first + VB)
        return carry

    lax.fori_loop(0, (live_count + 2 * VB - 1) // (2 * VB), block, 0)
    gridded[0] = total[:, :SUB].astype(BF16)
    gridded[1] = total[:, SUB:].astype(BF16)


def gather_kernel(facets, own, slabs, send, recv):
    me = lax.axis_index("facet")
    greet(facets)
    orders = [order[:0:-1] + order[:1] for order in routes(facets)]
    levels = len(orders[0])
    sent = []

    def copy_of(level, slab, part):
        bit = orders[part][level]
        source = slabs.at[slab, part] if slab else own.at[part]
        return remote(
            source, slabs.at[slab + bit, part],
            send.at[part, slab + bit], recv.at[part, slab + bit],
            "facet", flip(me, bit),
        )

    def post(level, slab, part):
        copy = copy_of(level, slab, part)
        copy.start()
        sent.append(copy)

    for level in range(levels):
        for part in range(2):
            post(level, 0, part)
    slabs[0] = own[...]
    held = [[0], [0]]
    for level in range(levels):
        for both in zip(*held):
            for part, slab in enumerate(both):
                copy_of(level, slab, part).wait_recv()
                for later in range(level + 1, levels):
                    post(later, slab + orders[part][level], part)
        held = [held[p] + [s + orders[p][level] for s in held[p]] for p in range(2)]
    for copy in sent:
        copy.wait_send()


def adjoint_kernel(facets, corners, everyone, left_table, right_table, turned_table, pieces, plane):
    cols = plane.shape[1] // 2
    chunk = pieces.shape[1]
    plane[...] = jnp.zeros_like(plane)

    def add_source(slab, carry):
        top = pl.multiple_of(corners[0, slab], STEP)
        left = pl.multiple_of(corners[1, slab], STEP)
        source = everyone[slab].reshape(2 * SUB, SUB)
        half = jnp.dot(left_table[...], source, preferred_element_type=F32)
        row = jnp.concatenate([half[:MC], half[MC:]], axis=1).astype(BF16)
        table = jnp.concatenate(
            [right_table[pl.ds(left, cols), :], turned_table[pl.ds(left, cols), :]], axis=0
        )
        window = lax.dot_general(row, table, (((1,), (1,)), ((), ())), preferred_element_type=F32)
        plane[pl.ds(top, MC), :] += window
        return carry

    lax.fori_loop(0, facets, add_source, 0, unroll=2)
    for piece in range(pieces.shape[0]):
        pieces[piece] = plane[piece * chunk : (piece + 1) * chunk, :].astype(BF16)


def line_kernel(groups, pieces, update, totals, landed, send, recv):
    me = lax.axis_index("sub")
    barrier = pltpu.get_barrier_semaphore()
    inner = (me > 0, me < groups - 1)
    ahead = ((me + 1) % groups, (me + groups - 1) % groups)
    behind = (ahead[1], ahead[0])
    for way in range(2):
        @pl.when(inner[way])
        def _():
            pl.semaphore_signal(
                barrier, inc=1, device_id={"sub": behind[way]}, device_id_type=MESH
            )
    between = jnp.logical_and(inner[0], inner[1])

    @pl.when(between)
    def _():
        pl.semaphore_wait(barrier, 2)

    @pl.when(jnp.logical_not(between))
    def _():
        pl.semaphore_wait(barrier, 1)

    cols = update.shape[3]
    size = pieces.shape[1]
    cut = (size // 2 + 15) // 16 * 16
    spans = (pl.ds(0, cut), pl.ds(cut, size - cut))

    def copy_of(source, way, chunk, part):
        return remote(
            source.at[chunk, spans[part]], landed.at[way, chunk, spans[part]],
            send.at[way, chunk, part], recv.at[way, chunk, part], "sub", ahead[way],
        )

    def plan(place):
        steps = []
        for way in range(2):
            depth = place if way == 0 else groups - 1 - place
            for turn in range(2 * (groups - 1 - depth)):
                chunk = turn // 2 if way else groups - 1 - turn // 2
                steps.append((turn + depth, depth, way, chunk, turn % 2))
        return sorted(steps)

    for place in range(groups):
        @pl.when(me == place)
        def _():
            for _, depth, way, chunk, part in plan(place):
                if depth == 0:
                    copy_of(pieces, way, chunk, part).start()
                    continue
                copy_of(pieces, way, chunk, part).wait_recv()
                totals[way, chunk, spans[part]] = (
                    pieces[chunk, spans[part]].astype(F32)
                    + landed[way, chunk, spans[part]].astype(F32)
                ).astype(BF16)
                copy_of(totals.at[way], way, chunk, part).start()
            for part in range(2):
                span = spans[part]
                value = pieces[place, span].astype(F32)
                for way in range(2):
                    if place != (0, groups - 1)[way]:
                        copy_of(pieces, way, place, part).wait_recv()
                        value = value + landed[way, place, span].astype(F32)
                update[0, 0, span] = value[:, :cols]
                update[0, 1, span] = value[:, cols:]
            for _, depth, way, chunk, part in plan(place):
                copy_of(pieces, way, chunk, part).wait_send()


def phases(facets):
    modulus = SUB * facets
    centred = np.arange(SUB) - SUB // 2
    base = np.exp(2j * np.pi * (np.outer(centred, centred) * facets % modulus) / modulus)
    turn = np.exp(2j * np.pi * (np.outer(np.arange(facets), centred) % modulus) / modulus)
    pair = lambda z: jnp.asarray(np.stack([z.real, z.imag]).astype(np.float32))
    return pair(base * MC ** (-0.5)), jnp.swapaxes(pair(turn), 0, 1)


def on_device(facet_spec, worker_of_subgrid, vis_count, bin_offsets, bin_fractions, observed):
    facets = lax.axis_size("facet")
    pos_v = lax.axis_size("sub")
    rows = facet_spec.shape[2]
    cols = facet_spec.shape[3]
    pad = (pos_v - 1) * STEP
    slots = bin_offsets.shape[2]
    base, turns = phases(facets)
    levels = len(bits_of(facets))
    slab_shape = (2, SUB, SUB)
    limit = 60 * 1024 * 1024
    slabs, left_adjoint, right, right_turned, corners = pl.pallas_call(
        functools.partial(transform_kernel, facets, pos_v),
        out_shape=(
            jax.ShapeDtypeStruct((facets,) + slab_shape, BF16),
            jax.ShapeDtypeStruct((2 * MC, 2 * SUB), BF16),
            jax.ShapeDtypeStruct((MC + 2 * pad, 2 * SUB), BF16),
            jax.ShapeDtypeStruct((MC + 2 * pad, 2 * SUB), BF16),
            jax.ShapeDtypeStruct((2, facets), jnp.int32),
        ),
        in_specs=[VMEM, VMEM, SMEM, VMEM],
        out_specs=(VMEM, VMEM, VMEM, VMEM, SMEM),
        scratch_shapes=[
            pltpu.VMEM((2 * SUB, 2 * MC), BF16),
            pltpu.SMEM(worker_of_subgrid.shape, jnp.int32),
        ],
        compiler_params=pltpu.CompilerParams(vmem_limit_bytes=limit),
        name="transform",
    )(base, turns, worker_of_subgrid, facet_spec)

    grid = pl.pallas_call(
        functools.partial(halve_kernel, facets),
        out_shape=jax.ShapeDtypeStruct(slab_shape, BF16),
        in_specs=[VMEM],
        out_specs=VMEM,
        scratch_shapes=[
            pltpu.VMEM((facets,) + slab_shape, BF16),
            pltpu.VMEM((levels, facets) + slab_shape, BF16),
            pltpu.SemaphoreType.DMA((2 * levels, facets)),
            pltpu.SemaphoreType.DMA((2 * levels, facets)),
        ],
        compiler_params=pltpu.CompilerParams(
            collective_id=0, has_side_effects=True, vmem_limit_bytes=limit
        ),
        name="sum_grids",
    )(slabs)

    residual, gridded = pl.pallas_call(
        vis_kernel,
        out_shape=(
            jax.ShapeDtypeStruct((1, 2, slots), F32),
            jax.ShapeDtypeStruct(slab_shape, BF16),
        ),
        in_specs=[SMEM, VMEM, VMEM, VMEM, VMEM],
        out_specs=(VMEM, VMEM),
        scratch_shapes=[
            pltpu.VMEM((2 * SUB, SUB), BF16),
            pltpu.VMEM((SUB, 2 * SUB), F32),
        ],
        compiler_params=pltpu.CompilerParams(vmem_limit_bytes=limit),
        name="visibilities",
    )(vis_count, grid, bin_offsets, bin_fractions, observed)

    everyone = pl.pallas_call(
        functools.partial(gather_kernel, facets),
        out_shape=jax.ShapeDtypeStruct((facets,) + slab_shape, BF16),
        in_specs=[VMEM],
        out_specs=VMEM,
        scratch_shapes=[
            pltpu.SemaphoreType.DMA((2, facets)),
            pltpu.SemaphoreType.DMA((2, facets)),
        ],
        compiler_params=pltpu.CompilerParams(
            collective_id=1, has_side_effects=True, vmem_limit_bytes=limit
        ),
        name="gather_grids",
    )(gridded)

    chunk = rows // pos_v
    pieces = pl.pallas_call(
        functools.partial(adjoint_kernel, facets),
        out_shape=jax.ShapeDtypeStruct((pos_v, chunk, 2 * cols), BF16),
        in_specs=[SMEM, VMEM, VMEM, VMEM, VMEM],
        out_specs=VMEM,
        scratch_shapes=[pltpu.VMEM((rows, 2 * cols), F32)],
        compiler_params=pltpu.CompilerParams(vmem_limit_bytes=limit),
        name="adjoint",
    )(corners, everyone, left_adjoint, right, right_turned)

    update = pl.pallas_call(
        functools.partial(line_kernel, pos_v),
        out_shape=jax.ShapeDtypeStruct((1, 2, chunk, cols), F32),
        in_specs=[VMEM],
        out_specs=VMEM,
        scratch_shapes=[
            pltpu.VMEM((2, pos_v, chunk, 2 * cols), BF16),
            pltpu.VMEM((2, pos_v, chunk, 2 * cols), BF16),
            pltpu.SemaphoreType.DMA((2, pos_v, 2)),
            pltpu.SemaphoreType.DMA((2, pos_v, 2)),
        ],
        compiler_params=pltpu.CompilerParams(
            collective_id=2, has_side_effects=True, vmem_limit_bytes=limit
        ),
        name="sum_pieces",
    )(pieces)
    return (residual, update)


def solution(mesh):
    placed = (
        P("facet", None, None, None),
        P(),
        P(("facet", "sub")),
        P(("facet", "sub"), None, None),
        P(("facet", "sub"), None, None),
        P(("facet", "sub"), None, None),
    )
    return jax.shard_map(
        on_device,
        mesh=mesh,
        in_specs=placed,
        out_specs=(P(("facet", "sub"), None, None), P("facet", None, "sub", None)),
        check_vma=False,
    )
```

profile of v0, /device:TPU:16, one launch (start us, length us, event | category | flops | bytes accessed | tf_op | source)
XLA Modules:
  0.0 95.6 jit_solution(10900867199242116797)
XLA Ops:
  0.6 2.5 %copy.10.spec = bf16[1,2,704,448]{3,2,1,0:T(8,128)(2,1)} copy(bf16[1,2,704,448]{2,3,1,0:T(8,128)(2,1)} %param.8) | data formatting | bytes 2523136 | tf_op args[0]
  3.1 11.7 %transform.1 = (bf16[8,2,256,256]{3,2,1,0:T(8,128)(2,1)}, bf16[512,512]{1,0:T(8,128)(2,1)}, bf16[640,512]{1,0:T(8,128)(2,1)}, bf16[640,512]{1,0:T(8,128)(2,1)}, s32[2,8]{1,0:T(2,128)}) custom-call(f32[2,256,256]{2,1,0:T(8,128)} %constant.4.clone.base, f32[8,2,256]{2,1,0:T(2,128)} %constant.11.turns, s32[32]{0:T(128)} %worker.1, ...), custom_call_target="tpu_custom_call" | custom-call | tf_op jit(solution)/shard_map/transform/pallas_call | solution.py:363
  14.8 16.6 %sum_grids.1.grid = bf16[2,256,256]{2,1,0:T(8,128)(2,1)} custom-call(bf16[8,2,256,256]{3,2,1,0:T(8,128)(2,1)} %get-tuple-element.9.slabs), custom_call_target="tpu_custom_call" | custom-call | tf_op jit(solution)/shard_map/sum_grids/pallas_call | solution.py:382
  32.1 3.3 %visibilities.1 = (f32[1,2,8192]{2,1,0:T(2,128)}, bf16[2,256,256]{2,1,0:T(8,128)(2,1)}) custom-call(s32[1]{0:T(128)S(6)} %copy.12.count, bf16[2,256,256]{2,1,0:T(8,128)(2,1)} %sum_grids.1.grid, s32[1,2,8192]{2,1,0:T(2,128)} %offsets.1, f32[1,2,8192]{2,1,0:T(2,128)} %fractions.1, f32[1,2,8192]{2,1,0:T(2,128)} %observed.1), custom_call_target="tpu_custom_call" | custom-call | tf_op jit(solution)/shard_map/visibilities/pallas_call | solution.py:399
  35.4 24.1 %gather_grids.1.everyone = bf16[8,2,256,256]{3,2,1,0:T(8,128)(2,1)} custom-call(bf16[2,256,256]{2,1,0:T(8,128)(2,1)} %get-tuple-element.12.own), custom_call_target="tpu_custom_call" | custom-call | tf_op jit(solution)/shard_map/gather_grids/pallas_call | solution.py:415
  59.5 8.3 %adjoint.1.pieces = bf16[4,176,896]{2,1,0:T(8,128)(2,1)} custom-call(s32[2,8]{1,0:T(2,128)} %get-tuple-element.11.corners, bf16[8,2,256,256]{3,2,1,0:T(8,128)(2,1)} %gather_grids.1.everyone, bf16[512,512]{1,0:T(8,128)(2,1)} %get-tuple-element.13.left_table, bf16[640,512]{1,0:T(8,128)(2,1)} %get-tuple-element.14.right_table, ...), custom_call_target="tpu_custom_call" | custom-call | tf_op jit(solution)/shard_map/adjoint/pallas_call | solution.py:431
  67.8 25.8 %sum_pieces.1 = f32[1,2,176,448]{3,2,1,0:T(8,128)} custom-call(bf16[4,176,896]{2,1,0:T(8,128)(2,1)} %adjoint.1.pieces), custom_call_target="tpu_custom_call" | custom-call | tf_op jit(solution)/shard_map/sum_pieces/pallas_call | solution.py:441
  93.6 2.0 %copy.13 = f32[1,2,176,448]{3,2,1,0:T(8,128)} copy(f32[1,2,176,448]{3,2,1,0:T(8,128)} %sum_pieces.1) | data formatting | bytes 1261568
where the time goes:
time: 95.9 us; the launch traced here: 95.6 us
  Pallas kernels  89.8 us (94%)
  local copies, waits for them, and re-layouts  4.52 us (5%)
  between operations  1.31 us (1%)
    pallas_call x1, Pallas kernels, on_device(): pl.pallas_call(functools.partial(line_kernel, pos_v), out_shape=jax.Shape...  25.8 us
    pallas_call x1, Pallas kernels, on_device(): pl.pallas_call(functools.partial(gather_kernel, facets), out_shape=jax.Sh...  24.1 us
    pallas_call x1, Pallas kernels, on_device(): pl.pallas_call(functools.partial(halve_kernel, facets), out_shape=jax.Sha...  16.6 us
    pallas_call x1, Pallas kernels, on_device(): pl.pallas_call(functools.partial(transform_kernel, facets, pos_v), out_sh...  11.7 us
    pallas_call x1, Pallas kernels, on_device(): pl.pallas_call(functools.partial(adjoint_kernel, facets), out_shape=jax.S...  8.26 us
    unnamed x2, local copies, waits for them, and re-layouts  4.52 us
    pallas_call x1, Pallas kernels, on_device(): pl.pallas_call(vis_kernel, out_shape=(jax.ShapeDtypeStruct((1, 2, slots),...  3.32 us

commit v1 on v0

--- a/solution.py
+++ b/solution.py
@@ -349,7 +349,7 @@
     return pair(base * MC ** (-0.5)), jnp.swapaxes(pair(turn), 0, 1)
 
 
-def on_device(facet_spec, worker_of_subgrid, vis_count, bin_offsets, bin_fractions, observed):
+def staged_path(facet_spec, worker_of_subgrid, vis_count, bin_offsets, bin_fractions, observed):
     facets = lax.axis_size("facet")
     pos_v = lax.axis_size("sub")
     rows = facet_spec.shape[2]
@@ -457,6 +457,442 @@
     return (residual, update)
 
 
+CELLS = 16
+FILL = 4
+
+
+def spread(values, groups):
+    zero = jnp.zeros_like(values)
+    rows = [jnp.where(groups == cell, values, zero) for cell in range(SUB // CELLS)]
+    return jnp.concatenate(rows, axis=0)
+
+
+def compact(offsets, fractions):
+    row = lax.broadcasted_iota(jnp.int32, (CELLS, offsets.shape[1]), 0)
+    ahead = (row - offsets) & (CELLS - 1)
+    scale = math.sqrt(math.log2(math.e)) * 9.0 / KS
+    distance = (ahead.astype(F32) - (0.5 * KS - 1.0) - fractions) * scale
+    values = jnp.where(ahead < KS, jnp.exp2(-1.0 - distance * distance), 0.0)
+    return values.astype(BF16), (offsets + ahead) // CELLS
+
+
+def gather_cells(product, bits):
+    parts = [product[i * CELLS : (i + 1) * CELLS] for i in range(SUB // CELLS)]
+    for bit in bits:
+        parts = [jnp.where(bit, b, a) for a, b in zip(parts[::2], parts[1::2])]
+    return parts[0]
+
+
+def row_spans(size):
+    step = (size // FILL + 15) // 16 * 16
+    return [(at, min(step, size - at)) for at in range(0, size, step)]
+
+
+def corners_kernel(facets, pos_v, margin, worker, corners, holder):
+    me = lax.axis_index("facet")
+    rank = lax.axis_index("sub")
+
+    def note(subgrid, carry):
+        holder[worker[subgrid]] = subgrid
+        return carry
+
+    lax.fori_loop(0, worker.shape[0], note, 0, unroll=8)
+    for slab in range(facets):
+        member = me
+        for bit in bits_of(facets):
+            member = flip(member, bit) if slab & bit else member
+        subgrid = holder[member * pos_v + rank]
+        top, left = subgrid // pos_v, subgrid % pos_v
+        corners[0, slab] = top
+        corners[1, slab] = left
+        corners[2, slab] = (margin - top * STEP) // CELLS
+
+
+def fused_kernel(
+    facets, pos_v, block, base, turns, corners, count, spec, offsets, fractions, observed,
+    residual, update, left_table, right_table, placed_table, views, out_core, in_core,
+    out_x, out_y, in_x, in_y, kept, grid, u_dense, v_values, v_groups, total, slabs, padded,
+    staged, landed, core_sems, x_sems, y_sems, gather_sems, line_sems
+):
+    me = lax.axis_index("facet")
+    rank = lax.axis_index("sub")
+    cols, rows = spec.shape[2], spec.shape[3]
+    slots = offsets.shape[2]
+    margin = rows - MC
+    core, axis_x, axis_y = 1, 2, 4
+    here = {bit: flip(me, bit) for bit in (core, axis_x, axis_y)}
+
+    barrier = pltpu.get_barrier_semaphore()
+    for bit in here:
+        pl.semaphore_signal(barrier, inc=1, device_id={"facet": here[bit]}, device_id_type=MESH)
+    inner = (rank > 0, rank < pos_v - 1)
+    ahead = ((rank + 1) % pos_v, (rank + pos_v - 1) % pos_v)
+    for way in range(2):
+        @pl.when(inner[way])
+        def _():
+            pl.semaphore_signal(
+                barrier, inc=1, device_id={"sub": ahead[1 - way]}, device_id_type=MESH
+            )
+
+    def turned(facet):
+        turn = turns[facet]
+        real, imag = turn[0:1], turn[1:2]
+        return (base[0] * real - base[1] * imag, base[0] * imag + base[1] * real)
+
+    def quarters(table, real, imag, flipped_first):
+        table[:MC, :SUB] = real.astype(BF16)
+        table[MC:, SUB:] = real.astype(BF16)
+        low, high = (-imag, imag) if flipped_first else (imag, -imag)
+        table[:MC, SUB:] = low.astype(BF16)
+        table[MC:, :SUB] = high.astype(BF16)
+
+    real, imag = turned(me)
+    quarters(left_table, real, imag, False)
+    real, imag = turned((5 * me + 3) % facets)
+    b_real, b_imag = real.T, imag.T
+    quarters(right_table, b_real, b_imag, True)
+    for part in range(2):
+        even, odd = spec[0, part], spec[0, part, :, STEP:]
+        for top in range(views.shape[0]):
+            at = top // 2 * 2 * STEP
+            view = (odd if top % 2 else even)[:, at : at + MC]
+            views[top, part] = view.reshape(cols // STEP, STEP, MC)
+
+    @pl.when(jnp.logical_and(inner[0], inner[1]))
+    def _():
+        pl.semaphore_wait(barrier, 5)
+
+    @pl.when(jnp.logical_not(jnp.logical_and(inner[0], inner[1])))
+    def _():
+        pl.semaphore_wait(barrier, 4)
+
+    sent = []
+
+    def post(source, target, sems, index, bit):
+        send, recv = sems
+        copy = remote(source, target, send.at[index], recv.at[index], "facet", here[bit])
+        copy.start()
+        sent.append(copy)
+
+    def arrive(source, target, sems, index, bit):
+        send, recv = sems
+        remote(source, target, send.at[index], recv.at[index], "facet", here[bit]).wait_recv()
+
+    def contribution(slab):
+        top, left = corners[0, slab], corners[1, slab]
+        window = jnp.concatenate(
+            [
+                jnp.concatenate([views[top, part, left + i] for i in range(MC // STEP)], axis=0)
+                for part in range(2)
+            ],
+            axis=1,
+        )
+        half = jnp.dot(window, left_table[...], preferred_element_type=F32).astype(BF16)
+        half = jnp.concatenate([half[:, :SUB], half[:, SUB:]], axis=0)
+        return jnp.dot(right_table[...], half, preferred_element_type=F32)
+
+    def to_partner(slab):
+        value = contribution(slab)
+        out_core[slab // 2] = value.astype(BF16).reshape(2, SUB, SUB)
+        post(out_core.at[slab // 2], in_core.at[slab // 2], core_sems, slab // 2, core)
+
+    def own(slab):
+        value = contribution(slab).reshape(2, SUB, SUB)
+        arrive(out_core.at[slab // 2], in_core.at[slab // 2], core_sems, slab // 2, core)
+        return value + in_core[slab // 2].astype(F32)
+
+    def send_x(index, value):
+        out_x[index] = value.astype(BF16)
+        post(out_x.at[index], in_x.at[index], x_sems, index, axis_x)
+
+    def send_y(index, value):
+        out_y[index] = value.astype(BF16)
+        post(out_y.at[index], in_y.at[index], y_sems, index, axis_y)
+
+    def from_x(index):
+        arrive(out_x.at[index], in_x.at[index], x_sems, index, axis_x)
+        return in_x[index].astype(F32)
+
+    def from_y(index):
+        arrive(out_y.at[index], in_y.at[index], y_sems, index, axis_y)
+        return in_y[index].astype(F32)
+
+    to_partner(7)
+    to_partner(3)
+    to_partner(5)
+    value = own(6)
+    send_x(0, value[0])
+    send_y(0, value[1])
+    value = own(2)
+    send_x(1, value[0])
+    kept[0] = value[1]
+    value = own(4)
+    send_y(1, value[1])
+    kept[1] = value[0]
+    to_partner(1)
+    value = own(0)
+    kept[2] = value[0]
+    kept[3] = value[1]
+
+    def place(table, first, second):
+        blank = jnp.zeros((SUB, cols * 2 - MC), F32)
+        first = jnp.concatenate([first, blank], axis=1)
+        second = pltpu.roll(jnp.concatenate([second, blank], axis=1), cols, 1)
+        value = first + second
+        for left in range(pos_v):
+            moved = pltpu.roll(value, left * STEP, 1) if left else value
+            placed_table[left, table * SUB : (table + 1) * SUB] = moved.astype(BF16)
+
+    place(0, b_real, -b_imag)
+    place(1, b_imag, b_real)
+    send_x(2, kept[0] + from_y(0))
+    send_y(2, kept[1] + from_x(0))
+
+    def prepare(index, carry):
+        span = pl.ds(pl.multiple_of(index * block, block), block)
+        values, groups = compact(offsets[0, 0:1, span], fractions[0, 0:1, span])
+        u_dense[:, span] = spread(values, groups.astype(jnp.int16))
+        values, groups = compact(offsets[0, 1:2, span], fractions[0, 1:2, span])
+        v_values[:, span] = values.astype(F32)
+        v_groups[:, span] = groups
+        return carry
+
+    lax.fori_loop(0, slots // block, prepare, 0)
+
+    def clear(slab, carry):
+        blank = jnp.zeros((margin // CELLS, CELLS, 2 * cols), BF16)
+        padded[slab, : margin // CELLS] = blank
+        padded[slab, (margin + MC) // CELLS :] = blank
+        return carry
+
+    lax.fori_loop(0, facets, clear, 0)
+    total[...] = jnp.zeros_like(total)
+
+    grid[:SUB] = (kept[2] + from_x(1) + from_y(2)).astype(BF16)
+    grid[SUB:] = (kept[3] + from_y(1) + from_x(2)).astype(BF16)
+
+    live_count = count[0]
+
+    def visit(index, carry):
+        first = pl.multiple_of(index * block, block)
+        span = pl.ds(first, block)
+        u_weights = u_dense[:, span]
+        values, groups = v_values[:, span], v_groups[:, span]
+        short = groups.astype(jnp.int16)
+        product = jnp.dot(grid[...], u_weights, preferred_element_type=F32)
+        bits = [(groups & bit) != 0 for bit in bits_of(SUB // CELLS)]
+        live = first + lax.broadcasted_iota(jnp.int32, (1, block), 1) < live_count
+        weighted = []
+        for part in range(2):
+            cells = gather_cells(product[part * SUB : (part + 1) * SUB], bits)
+            model = jnp.sum(cells * values, axis=0, keepdims=True)
+            row = jnp.where(live, observed[0, part : part + 1, span] - model, 0.0)
+            residual[0, part : part + 1, span] = row
+            weighted.append(spread((row * values).astype(BF16), short))
+        total[...] += lax.dot_general(
+            u_weights,
+            jnp.concatenate(weighted, axis=0),
+            (((1,), (1,)), ((), ())),
+            preferred_element_type=F32,
+        )
+        return carry
+
+    lax.fori_loop(0, slots // block, visit, 0)
+    for part in range(2):
+        slabs[0, part] = total[:, part * SUB : (part + 1) * SUB].astype(BF16)
+
+    def share(slab, part, bit):
+        source, target = slabs.at[slab, part], slabs.at[slab + bit, part]
+        send, recv = gather_sems
+        copy = remote(
+            source, target, send.at[slab + bit, part], recv.at[slab + bit, part],
+            "facet", here[bit],
+        )
+        copy.start()
+        sent.append(copy)
+
+    def shared(slab, part):
+        bit = slab & -slab
+        send, recv = gather_sems
+        remote(
+            slabs.at[slab, part], slabs.at[slab, part], send.at[slab, part],
+            recv.at[slab, part], "facet", here[bit],
+        ).wait_recv()
+
+    def adjoint(slab):
+        source = slabs[slab].reshape(2 * SUB, SUB)
+        half = jnp.dot(left_table[...], source, preferred_element_type=F32).astype(BF16)
+        half = jnp.concatenate([half[:MC], half[MC:]], axis=1)
+        window = jnp.dot(half, placed_table[corners[1, slab]], preferred_element_type=F32)
+        window = window.astype(BF16).reshape(MC // CELLS, CELLS, 2 * cols)
+        padded[slab, margin // CELLS : (margin + MC) // CELLS] = window
+
+    share(0, 0, axis_x)
+    share(0, 1, axis_y)
+    share(0, 0, core)
+    share(0, 1, core)
+    share(0, 1, axis_x)
+    share(0, 0, axis_y)
+    adjoint(0)
+    shared(1, 0)
+    shared(1, 1)
+    adjoint(1)
+    shared(2, 0)
+    share(2, 0, axis_y)
+    share(2, 0, core)
+    shared(4, 1)
+    share(4, 1, axis_x)
+    share(4, 1, core)
+    shared(2, 1)
+    share(2, 1, core)
+    shared(4, 0)
+    share(4, 0, core)
+    adjoint(2)
+    adjoint(4)
+    shared(3, 0)
+    shared(3, 1)
+    adjoint(3)
+    shared(6, 0)
+    share(6, 0, core)
+    shared(6, 1)
+    share(6, 1, core)
+    shared(5, 0)
+    shared(5, 1)
+    adjoint(5)
+    adjoint(6)
+    shared(7, 0)
+    shared(7, 1)
+    adjoint(7)
+
+    piece = rows // pos_v
+    spans = row_spans(piece)
+    starts = [corners[2, slab] for slab in range(facets)]
+
+    def own_rows(chunk, part):
+        at, size = spans[part]
+        value = jnp.zeros((size, 2 * cols), F32)
+        for slab in range(facets):
+            begin = starts[slab] + (chunk * piece + at) // CELLS
+            pick = [padded[slab, begin + i] for i in range(size // CELLS)]
+            value = value + jnp.concatenate(pick, axis=0).astype(F32)
+        return value
+
+    def line_copy(way, chunk, part):
+        at, size = spans[part]
+        send, recv = line_sems
+        return remote(
+            staged.at[chunk, pl.ds(at, size)], landed.at[way, chunk, pl.ds(at, size)],
+            send.at[way, chunk, part], recv.at[way, chunk, part], "sub", ahead[way],
+        )
+
+    def plan(place):
+        steps = []
+        for way in range(2):
+            depth = place if way == 0 else pos_v - 1 - place
+            for turn in range(len(spans) * (pos_v - 1 - depth)):
+                chunk = turn // len(spans)
+                chunk = chunk if way else pos_v - 1 - chunk
+                steps.append((turn + depth, depth, way, chunk, turn % len(spans)))
+        return sorted(steps)
+
+    for spot in range(pos_v):
+        @pl.when(rank == spot)
+        def _():
+            for _, depth, way, chunk, part in plan(spot):
+                at, size = spans[part]
+                value = own_rows(chunk, part)
+                if depth:
+                    line_copy(way, chunk, part).wait_recv()
+                    value = value + landed[way, chunk, pl.ds(at, size)].astype(F32)
+                staged[chunk, pl.ds(at, size)] = value.astype(BF16)
+                line_copy(way, chunk, part).start()
+            for part, (at, size) in enumerate(spans):
+                value = own_rows(spot, part)
+                for way in range(2):
+                    if spot != (0, pos_v - 1)[way]:
+                        line_copy(way, spot, part).wait_recv()
+                        value = value + landed[way, spot, pl.ds(at, size)].astype(F32)
+                update[0, 0, pl.ds(at, size)] = value[:, :cols]
+                update[0, 1, pl.ds(at, size)] = value[:, cols:]
+            for _, depth, way, chunk, part in plan(spot):
+                line_copy(way, chunk, part).wait_send()
+
+    for copy in sent:
+        copy.wait_send()
+
+
+def fused(facet_spec, worker, vis_count, bin_offsets, bin_fractions, observed):
+    facets = lax.axis_size("facet")
+    pos_v = lax.axis_size("sub")
+    rows, cols = facet_spec.shape[2:]
+    slots = bin_offsets.shape[2]
+    block = math.gcd(slots, 2048)
+    base, turns = phases(facets)
+    piece = rows // pos_v
+    parts = len(row_spans(piece))
+    dma = pltpu.SemaphoreType.DMA
+    pair = lambda *shape: (dma(shape), dma(shape))
+    corners = pl.pallas_call(
+        functools.partial(corners_kernel, facets, pos_v, rows - MC),
+        out_shape=jax.ShapeDtypeStruct((3, facets), jnp.int32),
+        in_specs=[SMEM],
+        out_specs=SMEM,
+        scratch_shapes=[pltpu.SMEM(worker.shape, jnp.int32)],
+        name="corners",
+    )(worker)
+    return pl.pallas_call(
+        functools.partial(fused_kernel, facets, pos_v, block),
+        out_shape=(
+            jax.ShapeDtypeStruct((1, 2, slots), F32),
+            jax.ShapeDtypeStruct((1, 2, piece, cols), F32),
+        ),
+        in_specs=[VMEM, VMEM, SMEM, SMEM, VMEM, VMEM, VMEM, VMEM],
+        out_specs=(VMEM, VMEM),
+        scratch_shapes=[
+            pltpu.VMEM((2 * MC, 2 * SUB), BF16),
+            pltpu.VMEM((2 * SUB, 2 * MC), BF16),
+            pltpu.VMEM((pos_v, 2 * SUB, 2 * cols), BF16),
+            pltpu.VMEM(((rows - MC) // STEP + 1, 2, cols // STEP, STEP, MC), BF16),
+            pltpu.VMEM((facets // 2, 2, SUB, SUB), BF16),
+            pltpu.VMEM((facets // 2, 2, SUB, SUB), BF16),
+            pltpu.VMEM((3, SUB, SUB), BF16),
+            pltpu.VMEM((3, SUB, SUB), BF16),
+            pltpu.VMEM((3, SUB, SUB), BF16),
+            pltpu.VMEM((3, SUB, SUB), BF16),
+            pltpu.VMEM((4, SUB, SUB), F32),
+            pltpu.VMEM((2 * SUB, SUB), BF16),
+            pltpu.VMEM((SUB, slots), BF16),
+            pltpu.VMEM((CELLS, slots), F32),
+            pltpu.VMEM((CELLS, slots), jnp.int32),
+            pltpu.VMEM((SUB, 2 * SUB), F32),
+            pltpu.VMEM((facets, 2, SUB, SUB), BF16),
+            pltpu.VMEM((facets, (2 * rows - MC) // CELLS, CELLS, 2 * cols), BF16),
+            pltpu.VMEM((pos_v, piece, 2 * cols), BF16),
+            pltpu.VMEM((2, pos_v, piece, 2 * cols), BF16),
+            pair(facets // 2),
+            pair(3),
+            pair(3),
+            pair(facets, 2),
+            pair(2, pos_v, parts),
+        ],
+        compiler_params=pltpu.CompilerParams(
+            collective_id=3, has_side_effects=True, vmem_limit_bytes=60 * 1024 * 1024
+        ),
+        name="everything",
+    )(
+        base, turns, corners, vis_count, jnp.swapaxes(facet_spec, 2, 3),
+        bin_offsets, bin_fractions, observed,
+    )
+
+
+def on_device(facet_spec, *rest):
+    facets = lax.axis_size("facet")
+    rows, cols = facet_spec.shape[2:]
+    padded_bytes = facets * (2 * rows - MC) * 2 * cols * 2
+    fits = len(bits_of(facets)) == 3 and padded_bytes <= 20 * 1024 * 1024
+    return (fused if fits else staged_path)(facet_spec, *rest)
+
+
 def solution(mesh):
     placed = (
         P("facet", None, None, None),

time: 95.9 us -> 65.4 us (0.68)
  Pallas kernels: 89.8 us -> 60.3 us
  local copies, waits for them, and re-layouts: 4.52 us -> 3.49 us
    pallas_call x6 -> x2, Pallas kernels: 89.8 us -> 60.3 us  [the longest x1 58.9 us: fused(): pl.pallas_call(functools.partial(fused_kernel, facets, pos_v, block), out...]
    unnamed x2, local copies, waits for them, and re-layouts: 4.52 us -> 3.49 us
where the time goes in v1:
time: 65.4 us; the launch traced here: 65.1 us
  Pallas kernels  60.3 us (92%)
  local copies, waits for them, and re-layouts  3.49 us (5%)
  between operations  1.29 us (2%)
    pallas_call x1, Pallas kernels, fused(): pl.pallas_call(functools.partial(fused_kernel, facets, pos_v, block), out...  58.9 us
    unnamed x2, local copies, waits for them, and re-layouts  3.49 us
    pallas_call x1, Pallas kernels, fused(): pl.pallas_call(functools.partial(corners_kernel, facets, pos_v, rows - MC...  1.45 us

profile of v1, /device:TPU:16, one launch (start us, length us, event | category | flops | bytes accessed | tf_op | source)
XLA Modules:
  0.0 65.1 jit_solution(3597912266438544494)
XLA Ops:
  1.3 1.4 %corners.1 = s32[3,8]{1,0:T(4,128)} custom-call(s32[32]{0:T(128)} %worker.1), custom_call_target="tpu_custom_call" | custom-call | tf_op jit(solution)/shard_map/corners/pallas_call | solution.py:835
  2.7 58.9 %everything.1 = (f32[1,2,8192]{2,1,0:T(2,128)}, f32[1,2,176,448]{3,2,1,0:T(8,128)}) custom-call(f32[2,256,256]{2,1,0:T(8,128)} %constant.4.clone.base, f32[8,2,256]{2,1,0:T(2,128)} %constant.11.turns, s32[3,8]{1,0:T(4,128)} %corners.1, s32[1]{0:T(128)S(6)} %copy.12.count, bf16[1,2,448,704]{3,2,1,0:T(8,128)(2,1)} %bitcast.1, s32[1,2,8192]{2,1,0:T(2,128)} %offsets.1, ...), custom_call_target="tpu_custom_call" | custom-call | tf_op jit(solution)/shard_map/everything/pallas_call | solution.py:843
  61.6 1.5 %copy.13 = f32[1,2,8192]{2,1,0:T(2,128)} copy(f32[1,2,8192]{2,1,0:T(2,128)} %get-tuple-element.4) | data formatting | bytes 131072
  63.1 2.0 %copy.14 = f32[1,2,176,448]{3,2,1,0:T(8,128)} copy(f32[1,2,176,448]{3,2,1,0:T(8,128)} %get-tuple-element.5) | data formatting | bytes 1261568

commit v2 on v1

--- a/solution.py
+++ b/solution.py
@@ -488,28 +488,8 @@
     return [(at, min(step, size - at)) for at in range(0, size, step)]
 
 
-def corners_kernel(facets, pos_v, margin, worker, corners, holder):
-    me = lax.axis_index("facet")
-    rank = lax.axis_index("sub")
-
-    def note(subgrid, carry):
-        holder[worker[subgrid]] = subgrid
-        return carry
-
-    lax.fori_loop(0, worker.shape[0], note, 0, unroll=8)
-    for slab in range(facets):
-        member = me
-        for bit in bits_of(facets):
-            member = flip(member, bit) if slab & bit else member
-        subgrid = holder[member * pos_v + rank]
-        top, left = subgrid // pos_v, subgrid % pos_v
-        corners[0, slab] = top
-        corners[1, slab] = left
-        corners[2, slab] = (margin - top * STEP) // CELLS
-
-
 def fused_kernel(
-    facets, pos_v, block, base, turns, corners, count, spec, offsets, fractions, observed,
+    facets, pos_v, block, base, turns, worker, count, spec, offsets, fractions, observed,
     residual, update, left_table, right_table, placed_table, views, out_core, in_core,
     out_x, out_y, in_x, in_y, kept, grid, u_dense, v_values, v_groups, total, slabs, padded,
     staged, landed, core_sems, x_sems, y_sems, gather_sems, line_sems
@@ -534,6 +514,23 @@
                 barrier, inc=1, device_id={"sub": ahead[1 - way]}, device_id_type=MESH
             )
 
+    wanted = []
+    for slab in range(facets):
+        member = me
+        for bit in bits_of(facets):
+            member = flip(member, bit) if slab & bit else member
+        wanted.append(member * pos_v + rank)
+
+    def note(subgrid, found):
+        at = worker[subgrid]
+        return tuple(jnp.where(at == w, subgrid, f) for w, f in zip(wanted, found))
+
+    found = lax.fori_loop(
+        0, worker.shape[0], note, tuple(jnp.int32(0) for _ in wanted), unroll=8
+    )
+    tops = [subgrid // pos_v for subgrid in found]
+    lefts = [subgrid % pos_v for subgrid in found]
+
     def turned(facet):
         turn = turns[facet]
         real, imag = turn[0:1], turn[1:2]
@@ -579,7 +576,7 @@
         remote(source, target, send.at[index], recv.at[index], "facet", here[bit]).wait_recv()
 
     def contribution(slab):
-        top, left = corners[0, slab], corners[1, slab]
+        top, left = tops[slab], lefts[slab]
         window = jnp.concatenate(
             [
                 jnp.concatenate([views[top, part, left + i] for i in range(MC // STEP)], axis=0)
@@ -723,7 +720,7 @@
         source = slabs[slab].reshape(2 * SUB, SUB)
         half = jnp.dot(left_table[...], source, preferred_element_type=F32).astype(BF16)
         half = jnp.concatenate([half[:MC], half[MC:]], axis=1)
-        window = jnp.dot(half, placed_table[corners[1, slab]], preferred_element_type=F32)
+        window = jnp.dot(half, placed_table[lefts[slab]], preferred_element_type=F32)
         window = window.astype(BF16).reshape(MC // CELLS, CELLS, 2 * cols)
         padded[slab, margin // CELLS : (margin + MC) // CELLS] = window
 
@@ -766,7 +763,7 @@
 
     piece = rows // pos_v
     spans = row_spans(piece)
-    starts = [corners[2, slab] for slab in range(facets)]
+    starts = [(margin - top * STEP) // CELLS for top in tops]
 
     def own_rows(chunk, part):
         at, size = spans[part]
@@ -832,19 +829,11 @@
     parts = len(row_spans(piece))
     dma = pltpu.SemaphoreType.DMA
     pair = lambda *shape: (dma(shape), dma(shape))
-    corners = pl.pallas_call(
-        functools.partial(corners_kernel, facets, pos_v, rows - MC),
-        out_shape=jax.ShapeDtypeStruct((3, facets), jnp.int32),
-        in_specs=[SMEM],
-        out_specs=SMEM,
-        scratch_shapes=[pltpu.SMEM(worker.shape, jnp.int32)],
-        name="corners",
-    )(worker)
     return pl.pallas_call(
         functools.partial(fused_kernel, facets, pos_v, block),
         out_shape=(
-            jax.ShapeDtypeStruct((1, 2, slots), F32),
-            jax.ShapeDtypeStruct((1, 2, piece, cols), F32),
+            pltpu.VMEM((1, 2, slots), F32),
+            pltpu.VMEM((1, 2, piece, cols), F32),
         ),
         in_specs=[VMEM, VMEM, SMEM, SMEM, VMEM, VMEM, VMEM, VMEM],
         out_specs=(VMEM, VMEM),
@@ -876,11 +865,11 @@
             pair(2, pos_v, parts),
         ],
         compiler_params=pltpu.CompilerParams(
-            collective_id=3, has_side_effects=True, vmem_limit_bytes=60 * 1024 * 1024
+            collective_id=3, has_side_effects=True, vmem_limit_bytes=56 * 1024 * 1024
         ),
         name="everything",
     )(
-        base, turns, corners, vis_count, jnp.swapaxes(facet_spec, 2, 3),
+        base, turns, worker, vis_count, jnp.swapaxes(facet_spec, 2, 3),
         bin_offsets, bin_fractions, observed,
     )
 

time: 65.4 us -> 61.4 us (0.939)
  local copies, waits for them, and re-layouts: 3.49 us -> 1.49 us
  Pallas kernels: 60.3 us -> 58.4 us
    unnamed x2, local copies, waits for them, and re-layouts: 3.49 us -> 1.49 us
    pallas_call x1 -> x0, Pallas kernels: 1.45 us -> none  [fused(): pl.pallas_call(functools.partial(corners_kernel, facets, pos_v, rows - MC...]
where the time goes in v2:
time: 61.4 us; the launch traced here: 61.2 us
  Pallas kernels  58.4 us (95%)
  local copies, waits for them, and re-layouts  1.49 us (2%)
  between operations  1.29 us (2%)
    pallas_call x1, Pallas kernels, fused(): pl.pallas_call(functools.partial(fused_kernel, facets, pos_v, block), out...  58.4 us
    unnamed x2, local copies, waits for them, and re-layouts  1.49 us

profile of v2, /device:TPU:16, one launch (start us, length us, event | category | flops | bytes accessed | tf_op | source)
XLA Modules:
  0.0 61.2 jit_solution(3558017460526243306)
XLA Ops:
  1.3 58.4 %everything.1 = (f32[1,2,8192]{2,1,0:T(2,128)S(1)}, f32[1,2,176,448]{3,2,1,0:T(8,128)S(1)}) custom-call(f32[2,256,256]{2,1,0:T(8,128)} %constant.4.clone.base, f32[8,2,256]{2,1,0:T(2,128)} %constant.11.turns, s32[32]{0:T(128)} %worker.1, s32[1]{0:T(128)S(6)} %copy.14.count, bf16[1,2,448,704]{3,2,1,0:T(8,128)(2,1)} %bitcast.1, s32[1,2,8192]{2,1,0:T(2,128)} %offsets.1, ...), custom_call_target="tpu_custom_call" | custom-call | tf_op jit(solution)/shard_map/everything/pallas_call | solution.py:832
  59.7 0.6 %copy.12 = f32[1,2,8192]{2,1,0:T(2,128)} copy(f32[1,2,8192]{2,1,0:T(2,128)S(1)} %get-tuple-element.2) | data formatting | bytes 131072
  60.3 0.9 %copy.13 = f32[1,2,176,448]{3,2,1,0:T(8,128)} copy(f32[1,2,176,448]{3,2,1,0:T(8,128)S(1)} %get-tuple-element.3) | data formatting | bytes 1261568

commit v3 on v2

--- a/solution.py
+++ b/solution.py
@@ -598,38 +598,53 @@
         arrive(out_core.at[slab // 2], in_core.at[slab // 2], core_sems, slab // 2, core)
         return value + in_core[slab // 2].astype(F32)
 
-    def send_x(index, value):
-        out_x[index] = value.astype(BF16)
-        post(out_x.at[index], in_x.at[index], x_sems, index, axis_x)
-
-    def send_y(index, value):
-        out_y[index] = value.astype(BF16)
-        post(out_y.at[index], in_y.at[index], y_sems, index, axis_y)
-
-    def from_x(index):
-        arrive(out_x.at[index], in_x.at[index], x_sems, index, axis_x)
-        return in_x[index].astype(F32)
-
-    def from_y(index):
-        arrive(out_y.at[index], in_y.at[index], y_sems, index, axis_y)
-        return in_y[index].astype(F32)
+    half_rows = SUB // 2
+    halves = (slice(0, half_rows), slice(half_rows, SUB))
+    lanes = {axis_x: (out_x, in_x, x_sems), axis_y: (out_y, in_y, y_sems)}
+
+    def hold(bit, part, index, value):
+        lanes[bit][0][part, index] = value.astype(BF16)
+
+    def go(bit, part, index):
+        out, landing, sems = lanes[bit]
+        post(out.at[part, index], landing.at[part, index], sems, (part, index), bit)
+
+    def come(bit, part, index):
+        out, landing, sems = lanes[bit]
+        arrive(out.at[part, index], landing.at[part, index], sems, (part, index), bit)
+        return landing[part, index].astype(F32)
 
     to_partner(7)
     to_partner(3)
     to_partner(5)
     value = own(6)
-    send_x(0, value[0])
-    send_y(0, value[1])
-    value = own(2)
-    send_x(1, value[0])
-    kept[0] = value[1]
-    value = own(4)
-    send_y(1, value[1])
-    kept[1] = value[0]
+    for part in range(2):
+        for bit, half in ((axis_x, 0), (axis_y, 1)):
+            hold(bit, part, 0, value[part, halves[half]])
+            if part == 0:
+                go(bit, 0, 0)
+    for slab, bit, near, far, keep in ((2, axis_x, 0, 1, 0), (4, axis_y, 1, 0, 1)):
+        value = own(slab)
+        for part in range(2):
+            hold(bit, part, 1, value[part, halves[near]])
+            if part == 0:
+                go(bit, 0, 1)
+                go(bit, 1, 0)
+            kept[keep, part] = value[part, halves[far]]
     to_partner(1)
     value = own(0)
-    kept[2] = value[0]
-    kept[3] = value[1]
+    for part in range(2):
+        for half in range(2):
+            kept[2 + half, part] = value[part, halves[half]]
+
+    def turn_corner(part):
+        for bit, other, keep in ((axis_x, axis_y, 0), (axis_y, axis_x, 1)):
+            hold(bit, part, 2, kept[keep, part] + come(other, part, 0))
+            go(bit, part, 2)
+
+    turn_corner(0)
+    go(axis_x, 1, 1)
+    go(axis_y, 1, 1)
 
     def place(table, first, second):
         blank = jnp.zeros((SUB, cols * 2 - MC), F32)
@@ -642,8 +657,7 @@
 
     place(0, b_real, -b_imag)
     place(1, b_imag, b_real)
-    send_x(2, kept[0] + from_y(0))
-    send_y(2, kept[1] + from_x(0))
+    turn_corner(1)
 
     def prepare(index, carry):
         span = pl.ds(pl.multiple_of(index * block, block), block)
@@ -654,7 +668,7 @@
         v_groups[:, span] = groups
         return carry
 
-    lax.fori_loop(0, slots // block, prepare, 0)
+    lax.fori_loop(0, slots // block, prepare, 0, unroll=2)
 
     def clear(slab, carry):
         blank = jnp.zeros((margin // CELLS, CELLS, 2 * cols), BF16)
@@ -662,59 +676,52 @@
         padded[slab, (margin + MC) // CELLS :] = blank
         return carry
 
-    lax.fori_loop(0, facets, clear, 0)
     total[...] = jnp.zeros_like(total)
-
-    grid[:SUB] = (kept[2] + from_x(1) + from_y(2)).astype(BF16)
-    grid[SUB:] = (kept[3] + from_y(1) + from_x(2)).astype(BF16)
-
     live_count = count[0]
 
-    def visit(index, carry):
+    def visit(part, index, carry):
         first = pl.multiple_of(index * block, block)
         span = pl.ds(first, block)
         u_weights = u_dense[:, span]
         values, groups = v_values[:, span], v_groups[:, span]
-        short = groups.astype(jnp.int16)
-        product = jnp.dot(grid[...], u_weights, preferred_element_type=F32)
+        product = jnp.dot(grid[part], u_weights, preferred_element_type=F32)
         bits = [(groups & bit) != 0 for bit in bits_of(SUB // CELLS)]
         live = first + lax.broadcasted_iota(jnp.int32, (1, block), 1) < live_count
-        weighted = []
-        for part in range(2):
-            cells = gather_cells(product[part * SUB : (part + 1) * SUB], bits)
-            model = jnp.sum(cells * values, axis=0, keepdims=True)
-            row = jnp.where(live, observed[0, part : part + 1, span] - model, 0.0)
-            residual[0, part : part + 1, span] = row
-            weighted.append(spread((row * values).astype(BF16), short))
-        total[...] += lax.dot_general(
+        model = jnp.sum(gather_cells(product, bits) * values, axis=0, keepdims=True)
+        row = jnp.where(live, observed[0, part : part + 1, span] - model, 0.0)
+        residual[0, part : part + 1, span] = row
+        total[part] += lax.dot_general(
             u_weights,
-            jnp.concatenate(weighted, axis=0),
+            spread((row * values).astype(BF16), groups.astype(jnp.int16)),
             (((1,), (1,)), ((), ())),
             preferred_element_type=F32,
         )
         return carry
 
-    lax.fori_loop(0, slots // block, visit, 0)
-    for part in range(2):
-        slabs[0, part] = total[:, part * SUB : (part + 1) * SUB].astype(BF16)
-
-    def share(slab, part, bit):
-        source, target = slabs.at[slab, part], slabs.at[slab + bit, part]
+    def visibilities(part):
+        for bit, other, half in ((axis_x, axis_y, 0), (axis_y, axis_x, 1)):
+            value = kept[2 + half, part] + come(bit, part, 1) + come(other, part, 2)
+            grid[part, halves[half]] = value.astype(BF16)
+        lax.fori_loop(0, slots // block, functools.partial(visit, part), 0, unroll=True)
+        slabs[0, part] = total[part].astype(BF16)
+
+    def gathered(slab, part, bit, half):
         send, recv = gather_sems
-        copy = remote(
-            source, target, send.at[slab + bit, part], recv.at[slab + bit, part],
-            "facet", here[bit],
-        )
+        index = (slab + bit, part, half or 0)
+        rows_of = slice(None) if half is None else halves[half]
+        return remote(
+            slabs.at[slab, part, rows_of], slabs.at[slab + bit, part, rows_of],
+            send.at[index], recv.at[index], "facet", here[bit],
+        )
+
+    def share(slab, part, bit, half=None):
+        copy = gathered(slab, part, bit, half)
         copy.start()
         sent.append(copy)
 
-    def shared(slab, part):
+    def shared(slab, part, half=None):
         bit = slab & -slab
-        send, recv = gather_sems
-        remote(
-            slabs.at[slab, part], slabs.at[slab, part], send.at[slab, part],
-            recv.at[slab, part], "facet", here[bit],
-        ).wait_recv()
+        gathered(slab - bit, part, bit, half).wait_recv()
 
     def adjoint(slab):
         source = slabs[slab].reshape(2 * SUB, SUB)
@@ -724,42 +731,45 @@
         window = window.astype(BF16).reshape(MC // CELLS, CELLS, 2 * cols)
         padded[slab, margin // CELLS : (margin + MC) // CELLS] = window
 
-    share(0, 0, axis_x)
-    share(0, 1, axis_y)
-    share(0, 0, core)
-    share(0, 1, core)
-    share(0, 1, axis_x)
-    share(0, 0, axis_y)
+    for part in range(2):
+        visibilities(part)
+        for bit in (axis_x, axis_y, core):
+            share(0, part, bit)
+
+    def pass_on(part):
+        for slab, bit, half in ((axis_x, axis_y, 0), (axis_y, axis_x, 1)):
+            shared(slab, part)
+            share(slab, part, bit, half)
+            share(slab, part, core)
+
+    def pass_far(part):
+        for half in range(2):
+            bit = (axis_y, axis_x)[half]
+            gathered(6 - bit, part, bit, half).wait_recv()
+            share(6, part, core, half)
+
+    def complete(slab):
+        for part in range(2):
+            if slab == 7:
+                for half in range(2):
+                    shared(slab, part, half)
+            else:
+                shared(slab, part)
+        adjoint(slab)
+
     adjoint(0)
-    shared(1, 0)
-    shared(1, 1)
-    adjoint(1)
-    shared(2, 0)
-    share(2, 0, axis_y)
-    share(2, 0, core)
-    shared(4, 1)
-    share(4, 1, axis_x)
-    share(4, 1, core)
-    shared(2, 1)
-    share(2, 1, core)
-    shared(4, 0)
-    share(4, 0, core)
+    pass_on(0)
+    complete(1)
+    lax.fori_loop(0, facets, clear, 0)
+    pass_on(1)
     adjoint(2)
     adjoint(4)
-    shared(3, 0)
-    shared(3, 1)
-    adjoint(3)
-    shared(6, 0)
-    share(6, 0, core)
-    shared(6, 1)
-    share(6, 1, core)
-    shared(5, 0)
-    shared(5, 1)
-    adjoint(5)
+    pass_far(0)
+    complete(3)
+    pass_far(1)
+    complete(5)
     adjoint(6)
-    shared(7, 0)
-    shared(7, 1)
-    adjoint(7)
+    complete(7)
 
     piece = rows // pos_v
     spans = row_spans(piece)
@@ -844,24 +854,24 @@
             pltpu.VMEM(((rows - MC) // STEP + 1, 2, cols // STEP, STEP, MC), BF16),
             pltpu.VMEM((facets // 2, 2, SUB, SUB), BF16),
             pltpu.VMEM((facets // 2, 2, SUB, SUB), BF16),
-            pltpu.VMEM((3, SUB, SUB), BF16),
-            pltpu.VMEM((3, SUB, SUB), BF16),
-            pltpu.VMEM((3, SUB, SUB), BF16),
-            pltpu.VMEM((3, SUB, SUB), BF16),
-            pltpu.VMEM((4, SUB, SUB), F32),
-            pltpu.VMEM((2 * SUB, SUB), BF16),
+            pltpu.VMEM((2, 3, SUB // 2, SUB), BF16),
+            pltpu.VMEM((2, 3, SUB // 2, SUB), BF16),
+            pltpu.VMEM((2, 3, SUB // 2, SUB), BF16),
+            pltpu.VMEM((2, 3, SUB // 2, SUB), BF16),
+            pltpu.VMEM((4, 2, SUB // 2, SUB), F32),
+            pltpu.VMEM((2, SUB, SUB), BF16),
             pltpu.VMEM((SUB, slots), BF16),
             pltpu.VMEM((CELLS, slots), F32),
             pltpu.VMEM((CELLS, slots), jnp.int32),
-            pltpu.VMEM((SUB, 2 * SUB), F32),
+            pltpu.VMEM((2, SUB, SUB), F32),
             pltpu.VMEM((facets, 2, SUB, SUB), BF16),
             pltpu.VMEM((facets, (2 * rows - MC) // CELLS, CELLS, 2 * cols), BF16),
             pltpu.VMEM((pos_v, piece, 2 * cols), BF16),
             pltpu.VMEM((2, pos_v, piece, 2 * cols), BF16),
             pair(facets // 2),
-            pair(3),
-            pair(3),
-            pair(facets, 2),
+            pair(2, 3),
+            pair(2, 3),
+            pair(facets, 2, 2),
             pair(2, pos_v, parts),
         ],
         compiler_params=pltpu.CompilerParams(

time: 61.4 us -> 58.1 us (0.946)
  Pallas kernels: 58.4 us -> 55.2 us
    pallas_call x1, Pallas kernels: 58.4 us -> 55.2 us  [fused(): pl.pallas_call(functools.partial(fused_kernel, facets, pos_v, block), out...]
where the time goes in v3:
time: 58.1 us; the launch traced here: 57.9 us
  Pallas kernels  55.2 us (95%)
  local copies, waits for them, and re-layouts  1.49 us (3%)
  between operations  1.29 us (2%)
    pallas_call x1, Pallas kernels, fused(): pl.pallas_call(functools.partial(fused_kernel, facets, pos_v, block), out...  55.2 us
    unnamed x2, local copies, waits for them, and re-layouts  1.49 us

profile of v3, /device:TPU:16, one launch (start us, length us, event | category | flops | bytes accessed | tf_op | source)
XLA Modules:
  0.0 57.9 jit_solution(14199430161810926276)
XLA Ops:
  1.3 55.2 %everything.1 = (f32[1,2,8192]{2,1,0:T(2,128)S(1)}, f32[1,2,176,448]{3,2,1,0:T(8,128)S(1)}) custom-call(f32[2,256,256]{2,1,0:T(8,128)} %constant.4.clone.base, f32[8,2,256]{2,1,0:T(2,128)} %constant.11.turns, s32[32]{0:T(128)} %worker.1, s32[1]{0:T(128)S(6)} %copy.14.count, bf16[1,2,448,704]{3,2,1,0:T(8,128)(2,1)} %bitcast.1, s32[1,2,8192]{2,1,0:T(2,128)} %offsets.1, ...), custom_call_target="tpu_custom_call" | custom-call | tf_op jit(solution)/shard_map/everything/pallas_call | solution.py:842
  56.4 0.6 %copy.12 = f32[1,2,8192]{2,1,0:T(2,128)} copy(f32[1,2,8192]{2,1,0:T(2,128)S(1)} %get-tuple-element.2) | data formatting | bytes 131072
  57.1 0.9 %copy.13 = f32[1,2,176,448]{3,2,1,0:T(8,128)} copy(f32[1,2,176,448]{3,2,1,0:T(8,128)S(1)} %get-tuple-element.3) | data formatting | bytes 1261568

commit v4 on v3

--- a/solution.py
+++ b/solution.py
@@ -458,7 +458,7 @@
 
 
 CELLS = 16
-FILL = 4
+FILL = 3
 
 
 def spread(values, groups):
@@ -492,7 +492,8 @@
     facets, pos_v, block, base, turns, worker, count, spec, offsets, fractions, observed,
     residual, update, left_table, right_table, placed_table, views, out_core, in_core,
     out_x, out_y, in_x, in_y, kept, grid, u_dense, v_values, v_groups, total, slabs, padded,
-    staged, landed, core_sems, x_sems, y_sems, gather_sems, line_sems
+    staged, landed, guest_slabs, lone, extra, core_sems, x_sems, y_sems, gather_sems,
+    line_sems, guest_sems, hand_sems
 ):
     me = lax.axis_index("facet")
     rank = lax.axis_index("sub")
@@ -507,29 +508,31 @@
         pl.semaphore_signal(barrier, inc=1, device_id={"facet": here[bit]}, device_id_type=MESH)
     inner = (rank > 0, rank < pos_v - 1)
     ahead = ((rank + 1) % pos_v, (rank + pos_v - 1) % pos_v)
-    for way in range(2):
+    upper = 2 * rank // pos_v
+    for way, step in enumerate((-1, 1)):
         @pl.when(inner[way])
         def _():
             pl.semaphore_signal(
-                barrier, inc=1, device_id={"sub": ahead[1 - way]}, device_id_type=MESH
+                barrier, inc=1, device_id={"sub": rank + step}, device_id_type=MESH
             )
 
-    wanted = []
-    for slab in range(facets):
-        member = me
-        for bit in bits_of(facets):
-            member = flip(member, bit) if slab & bit else member
-        wanted.append(member * pos_v + rank)
-
-    def note(subgrid, found):
-        at = worker[subgrid]
-        return tuple(jnp.where(at == w, subgrid, f) for w, f in zip(wanted, found))
-
-    found = lax.fori_loop(
-        0, worker.shape[0], note, tuple(jnp.int32(0) for _ in wanted), unroll=8
-    )
-    tops = [subgrid // pos_v for subgrid in found]
-    lefts = [subgrid % pos_v for subgrid in found]
+    def corners_of(place):
+        wanted = []
+        for slab in range(facets):
+            member = me
+            for bit in bits_of(facets):
+                member = flip(member, bit) if slab & bit else member
+            wanted.append(member * pos_v + place)
+
+        def note(subgrid, found):
+            at = worker[subgrid]
+            return tuple(jnp.where(at == w, subgrid, f) for w, f in zip(wanted, found))
+
+        blank = tuple(jnp.int32(0) for _ in wanted)
+        found = lax.fori_loop(0, worker.shape[0], note, blank, unroll=8)
+        return [subgrid // pos_v for subgrid in found], [subgrid % pos_v for subgrid in found]
+
+    tops, lefts = corners_of(rank)
 
     def turned(facet):
         turn = turns[facet]
@@ -705,125 +708,219 @@
         lax.fori_loop(0, slots // block, functools.partial(visit, part), 0, unroll=True)
         slabs[0, part] = total[part].astype(BF16)
 
-    def gathered(slab, part, bit, half):
-        send, recv = gather_sems
-        index = (slab + bit, part, half or 0)
-        rows_of = slice(None) if half is None else halves[half]
+    class Ring:
+        def __init__(self, store, sems):
+            self.store, self.sems, self.sent = store, sems, []
+
+        def copy(self, slab, part, bit, half):
+            send, recv = self.sems
+            index = (slab + bit, part, half or 0)
+            rows_of = slice(None) if half is None else halves[half]
+            return remote(
+                self.store.at[slab, part, rows_of], self.store.at[slab + bit, part, rows_of],
+                send.at[index], recv.at[index], "facet", here[bit],
+            )
+
+        def share(self, slab, part, bit, half=None):
+            self.copy(slab, part, bit, half).start()
+            self.sent.append((slab, part, bit, half))
+
+        def shared(self, slab, part, half=None):
+            bit = slab & -slab
+            self.copy(slab - bit, part, bit, half).wait_recv()
+
+        def begin(self, part):
+            for bit in (axis_x, axis_y, core):
+                self.share(0, part, bit)
+
+        def pass_on(self, part):
+            for slab, bit, half in ((axis_x, axis_y, 0), (axis_y, axis_x, 1)):
+                self.shared(slab, part)
+                self.share(slab, part, bit, half)
+                self.share(slab, part, core)
+
+        def pass_far(self, part):
+            for half in range(2):
+                bit = (axis_y, axis_x)[half]
+                self.copy(6 - bit, part, bit, half).wait_recv()
+                self.share(6, part, core, half)
+
+        def complete(self, slab):
+            for part in range(2):
+                for half in range(2) if slab == 7 else (None,):
+                    self.shared(slab, part, half)
+
+        def window(self, slab, left):
+            source = self.store[slab].reshape(2 * SUB, SUB)
+            half = jnp.dot(left_table[...], source, preferred_element_type=F32).astype(BF16)
+            half = jnp.concatenate([half[:MC], half[MC:]], axis=1)
+            window = jnp.dot(half, placed_table[left], preferred_element_type=F32)
+            return window.astype(BF16).reshape(MC // CELLS, CELLS, 2 * cols)
+
+        def settle(self):
+            for item in self.sent:
+                self.copy(*item).wait_send()
+
+    ring = Ring(slabs, gather_sems)
+    guests = Ring(guest_slabs, guest_sems)
+    inside = slice(margin // CELLS, (margin + MC) // CELLS)
+
+    def hand_over(way, part):
+        send, recv = hand_sems
         return remote(
-            slabs.at[slab, part, rows_of], slabs.at[slab + bit, part, rows_of],
-            send.at[index], recv.at[index], "facet", here[bit],
+            slabs.at[0, part], guest_slabs.at[0, part], send.at[part], recv.at[part],
+            "sub", ahead[way],
         )
-
-    def share(slab, part, bit, half=None):
-        copy = gathered(slab, part, bit, half)
-        copy.start()
-        sent.append(copy)
-
-    def shared(slab, part, half=None):
-        bit = slab & -slab
-        gathered(slab - bit, part, bit, half).wait_recv()
-
-    def adjoint(slab):
-        source = slabs[slab].reshape(2 * SUB, SUB)
-        half = jnp.dot(left_table[...], source, preferred_element_type=F32).astype(BF16)
-        half = jnp.concatenate([half[:MC], half[MC:]], axis=1)
-        window = jnp.dot(half, placed_table[lefts[slab]], preferred_element_type=F32)
-        window = window.astype(BF16).reshape(MC // CELLS, CELLS, 2 * cols)
-        padded[slab, margin // CELLS : (margin + MC) // CELLS] = window
 
     for part in range(2):
         visibilities(part)
-        for bit in (axis_x, axis_y, core):
-            share(0, part, bit)
-
-    def pass_on(part):
-        for slab, bit, half in ((axis_x, axis_y, 0), (axis_y, axis_x, 1)):
-            shared(slab, part)
-            share(slab, part, bit, half)
-            share(slab, part, core)
-
-    def pass_far(part):
-        for half in range(2):
-            bit = (axis_y, axis_x)[half]
-            gathered(6 - bit, part, bit, half).wait_recv()
-            share(6, part, core, half)
-
-    def complete(slab):
-        for part in range(2):
-            if slab == 7:
-                for half in range(2):
-                    shared(slab, part, half)
-            else:
-                shared(slab, part)
-        adjoint(slab)
+        ring.begin(part)
+
+        for way, spot in enumerate((0, pos_v - 1)):
+            @pl.when(rank == spot)
+            def _():
+                hand_over(way, part).start()
+
+    def adjoint(slab):
+        padded[slab, inside] = ring.window(slab, lefts[slab])
 
     adjoint(0)
-    pass_on(0)
-    complete(1)
+    ring.pass_on(0)
+    ring.complete(1)
+    adjoint(1)
     lax.fori_loop(0, facets, clear, 0)
-    pass_on(1)
+    for slot in range(2):
+        lone[slot, : inside.start] = jnp.zeros((inside.start, CELLS, 2 * cols), BF16)
+        lone[slot, inside.stop :] = jnp.zeros((inside.start, CELLS, 2 * cols), BF16)
+    extra[...] = jnp.zeros_like(extra)
+    ring.pass_on(1)
     adjoint(2)
     adjoint(4)
-    pass_far(0)
-    complete(3)
-    pass_far(1)
-    complete(5)
+    ring.pass_far(0)
+    ring.complete(3)
+    adjoint(3)
+    ring.pass_far(1)
+
+    for way, spot in enumerate((1, pos_v - 2)):
+        @pl.when(rank == spot)
+        def _():
+            for part in range(2):
+                hand_over(way, part).wait_recv()
+                guests.begin(part)
+
+    ring.complete(5)
+    adjoint(5)
     adjoint(6)
-    complete(7)
+    ring.complete(7)
+    adjoint(7)
 
     piece = rows // pos_v
     spans = row_spans(piece)
     starts = [(margin - top * STEP) // CELLS for top in tops]
+    guest_place = upper * (pos_v - 1)
+    guest_tops, guest_lefts = corners_of(guest_place)
+
+    def guest(slab):
+        slot = slab % 2
+        lone[slot, inside] = guests.window(slab, guest_lefts[slab])
+        begin = (margin - guest_tops[slab] * STEP) // CELLS + rank * (piece // CELLS)
+        pick = [lone[slot, begin + i] for i in range(piece // CELLS)]
+        extra[...] += jnp.concatenate(pick, axis=0).astype(F32)
+
+    def guest_tasks():
+        def both(*calls):
+            def run():
+                for call, *args in calls:
+                    call(*args)
+            return run
+
+        return [
+            both((guests.pass_on, 0), (guest, 0)),
+            both((guests.complete, 1), (guest, 1)),
+            both((guests.pass_on, 1), (guest, 2)),
+            both((guest, 4),),
+            both((guests.pass_far, 0),),
+            both((guests.complete, 3), (guest, 3)),
+            both((guests.pass_far, 1),),
+            both((guests.complete, 5), (guest, 5)),
+            both((guest, 6),),
+            both((guests.complete, 7), (guest, 7)),
+        ]
 
     def own_rows(chunk, part):
         at, size = spans[part]
         value = jnp.zeros((size, 2 * cols), F32)
         for slab in range(facets):
-            begin = starts[slab] + (chunk * piece + at) // CELLS
+            begin = starts[slab] + chunk * (piece // CELLS) + at // CELLS
             pick = [padded[slab, begin + i] for i in range(size // CELLS)]
             value = value + jnp.concatenate(pick, axis=0).astype(F32)
         return value
 
     def line_copy(way, chunk, part):
-        at, size = spans[part]
+        rows_of = pl.ds(*spans[part])
         send, recv = line_sems
         return remote(
-            staged.at[chunk, pl.ds(at, size)], landed.at[way, chunk, pl.ds(at, size)],
+            staged.at[chunk, rows_of], landed.at[way, chunk, rows_of],
             send.at[way, chunk, part], recv.at[way, chunk, part], "sub", ahead[way],
         )
 
-    def plan(place):
+    def plan(place, mirrored):
         steps = []
         for way in range(2):
-            depth = place if way == 0 else pos_v - 1 - place
-            for turn in range(len(spans) * (pos_v - 1 - depth)):
-                chunk = turn // len(spans)
-                chunk = chunk if way else pos_v - 1 - chunk
-                steps.append((turn + depth, depth, way, chunk, turn % len(spans)))
+            depth = pos_v - 1 - place if way else place
+            chunks = range(place) if way else range(pos_v - 1, max(place, 1), -1)
+            for turn, (chunk, part) in enumerate((c, p) for c in chunks for p in range(len(spans))):
+                near = pos_v - 1 - chunk if mirrored else chunk
+                steps.append((turn + depth, depth, way, 1 - way if mirrored else way, near, part))
         return sorted(steps)
 
     for spot in range(pos_v):
+        mirrored = 2 * spot >= pos_v
+        place = pos_v - 1 - spot if mirrored else spot
+
         @pl.when(rank == spot)
         def _():
-            for _, depth, way, chunk, part in plan(spot):
-                at, size = spans[part]
+            first_sent = len(guests.sent)
+            tasks = guest_tasks() if place == 1 else []
+            budget, relays = len(tasks), 0
+            for _, depth, away, way, chunk, part in plan(place, mirrored):
+                rows_of = pl.ds(*spans[part])
                 value = own_rows(chunk, part)
                 if depth:
                     line_copy(way, chunk, part).wait_recv()
-                    value = value + landed[way, chunk, pl.ds(at, size)].astype(F32)
-                staged[chunk, pl.ds(at, size)] = value.astype(BF16)
+                    value = value + landed[way, chunk, rows_of].astype(F32)
+                staged[chunk, rows_of] = value.astype(BF16)
                 line_copy(way, chunk, part).start()
-            for part, (at, size) in enumerate(spans):
+                if away == 0:
+                    relays += 1
+                    while tasks and budget - len(tasks) < relays * budget // (2 * len(spans)):
+                        tasks.pop(0)()
+            for task in tasks:
+                task()
+            for part, span in enumerate(spans):
+                rows_of = pl.ds(*span)
                 value = own_rows(spot, part)
+                if place == 1:
+                    value = value + extra[rows_of]
                 for way in range(2):
-                    if spot != (0, pos_v - 1)[way]:
+                    if way != (1 if mirrored else 0) or place > 1:
                         line_copy(way, spot, part).wait_recv()
-                        value = value + landed[way, spot, pl.ds(at, size)].astype(F32)
-                update[0, 0, pl.ds(at, size)] = value[:, :cols]
-                update[0, 1, pl.ds(at, size)] = value[:, cols:]
-            for _, depth, way, chunk, part in plan(spot):
+                        value = value + landed[way, spot, rows_of].astype(F32)
+                update[0, 0, rows_of] = value[:, :cols]
+                update[0, 1, rows_of] = value[:, cols:]
+            for _, _, _, way, chunk, part in plan(place, mirrored):
                 line_copy(way, chunk, part).wait_send()
-
+            if place == 1:
+                for part in range(2):
+                    for bit in (axis_x, axis_y, core):
+                        guests.copy(0, part, bit, None).wait_send()
+                for item in guests.sent[first_sent:]:
+                    guests.copy(*item).wait_send()
+            if place == 0:
+                for part in range(2):
+                    hand_over(1 if mirrored else 0, part).wait_send()
+
+    ring.settle()
     for copy in sent:
         copy.wait_send()
 
@@ -868,11 +965,16 @@
             pltpu.VMEM((facets, (2 * rows - MC) // CELLS, CELLS, 2 * cols), BF16),
             pltpu.VMEM((pos_v, piece, 2 * cols), BF16),
             pltpu.VMEM((2, pos_v, piece, 2 * cols), BF16),
+            pltpu.VMEM((facets, 2, SUB, SUB), BF16),
+            pltpu.VMEM((2, (2 * rows - MC) // CELLS, CELLS, 2 * cols), BF16),
+            pltpu.VMEM((piece, 2 * cols), F32),
             pair(facets // 2),
             pair(2, 3),
             pair(2, 3),
             pair(facets, 2, 2),
             pair(2, pos_v, parts),
+            pair(facets, 2, 2),
+            pair(2),
         ],
         compiler_params=pltpu.CompilerParams(
             collective_id=3, has_side_effects=True, vmem_limit_bytes=56 * 1024 * 1024
@@ -888,7 +990,8 @@
     facets = lax.axis_size("facet")
     rows, cols = facet_spec.shape[2:]
     padded_bytes = facets * (2 * rows - MC) * 2 * cols * 2
-    fits = len(bits_of(facets)) == 3 and padded_bytes <= 20 * 1024 * 1024
+    line = lax.axis_size("sub")
+    fits = len(bits_of(facets)) == 3 and line >= 4 and line % 2 == 0 and padded_bytes <= 20 * 1024 * 1024
     return (fused if fits else staged_path)(facet_spec, *rest)
 
 

time: 58.1 us -> 57.7 us (level); the launches traced: 57.9 us -> 56.7 us
  Pallas kernels: 55.2 us -> 53.9 us
    pallas_call x1, Pallas kernels: 55.2 us -> 53.9 us  [fused(): pl.pallas_call(functools.partial(fused_kernel, facets, pos_v, block), out...]
where the time goes in v4:
time: 57.7 us; the launch traced here: 56.7 us
  Pallas kernels  53.9 us (93%)
  local copies, waits for them, and re-layouts  1.49 us (3%)
  between operations  1.29 us (2%)
    pallas_call x1, Pallas kernels, fused(): pl.pallas_call(functools.partial(fused_kernel, facets, pos_v, block), out...  53.9 us
    unnamed x2, local copies, waits for them, and re-layouts  1.49 us

profile of v4, /device:TPU:16, one launch (start us, length us, event | category | flops | bytes accessed | tf_op | source)
XLA Modules:
  0.0 56.7 jit_solution(14696735305248198151)
XLA Ops:
  1.3 53.9 %everything.1 = (f32[1,2,8192]{2,1,0:T(2,128)S(1)}, f32[1,2,176,448]{3,2,1,0:T(8,128)S(1)}) custom-call(f32[2,256,256]{2,1,0:T(8,128)} %constant.4.clone.base, f32[8,2,256]{2,1,0:T(2,128)} %constant.11.turns, s32[32]{0:T(128)} %worker.1, s32[1]{0:T(128)S(6)} %copy.14.count, bf16[1,2,448,704]{3,2,1,0:T(8,128)(2,1)} %bitcast.1, s32[1,2,8192]{2,1,0:T(2,128)} %offsets.1, ...), custom_call_target="tpu_custom_call" | custom-call | tf_op jit(solution)/shard_map/everything/pallas_call | solution.py:939
  55.2 0.6 %copy.12 = f32[1,2,8192]{2,1,0:T(2,128)} copy(f32[1,2,8192]{2,1,0:T(2,128)S(1)} %get-tuple-element.2) | data formatting | bytes 131072
  55.9 0.9 %copy.13 = f32[1,2,176,448]{3,2,1,0:T(8,128)} copy(f32[1,2,176,448]{3,2,1,0:T(8,128)S(1)} %get-tuple-element.3) | data formatting | bytes 1261568

commit v5 on v4

--- a/solution.py
+++ b/solution.py
@@ -492,7 +492,7 @@
     facets, pos_v, block, base, turns, worker, count, spec, offsets, fractions, observed,
     residual, update, left_table, right_table, placed_table, views, out_core, in_core,
     out_x, out_y, in_x, in_y, kept, grid, u_dense, v_values, v_groups, total, slabs, padded,
-    staged, landed, guest_slabs, lone, extra, core_sems, x_sems, y_sems, gather_sems,
+    staged, landed, guest_slabs, lone, extra, mine, core_sems, x_sems, y_sems, gather_sems,
     line_sems, guest_sems, hand_sems
 ):
     me = lax.axis_index("facet")
@@ -849,12 +849,17 @@
 
     def own_rows(chunk, part):
         at, size = spans[part]
-        value = jnp.zeros((size, 2 * cols), F32)
-        for slab in range(facets):
-            begin = starts[slab] + chunk * (piece // CELLS) + at // CELLS
-            pick = [padded[slab, begin + i] for i in range(size // CELLS)]
-            value = value + jnp.concatenate(pick, axis=0).astype(F32)
-        return value
+
+        def tile(index, carry):
+            value = jnp.zeros((CELLS, 2 * cols), F32)
+            for slab in range(facets):
+                begin = starts[slab] + chunk * (piece // CELLS) + at // CELLS
+                value = value + padded[slab, begin + index].astype(F32)
+            mine[index] = value
+            return carry
+
+        lax.fori_loop(0, size // CELLS, tile, 0)
+        return mine[: size // CELLS].reshape(size, 2 * cols)
 
     def line_copy(way, chunk, part):
         rows_of = pl.ds(*spans[part])
@@ -874,29 +879,45 @@
                 steps.append((turn + depth, depth, way, 1 - way if mirrored else way, near, part))
         return sorted(steps)
 
+    def relay(depth, way, chunk, part):
+        rows_of = pl.ds(*spans[part])
+        value = own_rows(chunk, part)
+        if depth:
+            line_copy(way, chunk, part).wait_recv()
+            value = value + landed[way, chunk, rows_of].astype(F32)
+        staged[chunk, rows_of] = value.astype(BF16)
+        line_copy(way, chunk, part).start()
+
+    sides = [2 * spot >= pos_v for spot in range(pos_v)]
+    places = [pos_v - 1 - spot if side else spot for spot, side in enumerate(sides)]
+    plans = [plan(place, side) for place, side in zip(places, sides)]
+    hosts = jnp.logical_or(rank == 1, rank == pos_v - 2)
+    first_sent = len(guests.sent)
+    tasks = guest_tasks()
+    budget, relays = len(tasks), 0
+    for step in range(max(len(steps) for steps in plans)):
+        for spot in range(pos_v):
+            if step < len(plans[spot]):
+                @pl.when(rank == spot)
+                def _():
+                    _, depth, _, *rest = plans[spot][step]
+                    relay(depth, *rest)
+        if step < len(plans[1]) and plans[1][step][2] == 0:
+            relays += 1
+            due = relays * budget // (2 * len(spans)) - (budget - len(tasks))
+
+            @pl.when(hosts)
+            def _():
+                for task in tasks[:due]:
+                    task()
+
+            tasks = tasks[due:]
+
     for spot in range(pos_v):
-        mirrored = 2 * spot >= pos_v
-        place = pos_v - 1 - spot if mirrored else spot
+        mirrored, place = sides[spot], places[spot]
 
         @pl.when(rank == spot)
         def _():
-            first_sent = len(guests.sent)
-            tasks = guest_tasks() if place == 1 else []
-            budget, relays = len(tasks), 0
-            for _, depth, away, way, chunk, part in plan(place, mirrored):
-                rows_of = pl.ds(*spans[part])
-                value = own_rows(chunk, part)
-                if depth:
-                    line_copy(way, chunk, part).wait_recv()
-                    value = value + landed[way, chunk, rows_of].astype(F32)
-                staged[chunk, rows_of] = value.astype(BF16)
-                line_copy(way, chunk, part).start()
-                if away == 0:
-                    relays += 1
-                    while tasks and budget - len(tasks) < relays * budget // (2 * len(spans)):
-                        tasks.pop(0)()
-            for task in tasks:
-                task()
             for part, span in enumerate(spans):
                 rows_of = pl.ds(*span)
                 value = own_rows(spot, part)
@@ -908,17 +929,19 @@
                         value = value + landed[way, spot, rows_of].astype(F32)
                 update[0, 0, rows_of] = value[:, :cols]
                 update[0, 1, rows_of] = value[:, cols:]
-            for _, _, _, way, chunk, part in plan(place, mirrored):
+            for _, _, _, way, chunk, part in plans[spot]:
                 line_copy(way, chunk, part).wait_send()
-            if place == 1:
-                for part in range(2):
-                    for bit in (axis_x, axis_y, core):
-                        guests.copy(0, part, bit, None).wait_send()
-                for item in guests.sent[first_sent:]:
-                    guests.copy(*item).wait_send()
             if place == 0:
                 for part in range(2):
                     hand_over(1 if mirrored else 0, part).wait_send()
+
+    @pl.when(hosts)
+    def _():
+        for part in range(2):
+            for bit in (axis_x, axis_y, core):
+                guests.copy(0, part, bit, None).wait_send()
+        for item in guests.sent[first_sent:]:
+            guests.copy(*item).wait_send()
 
     ring.settle()
     for copy in sent:
@@ -968,6 +991,7 @@
             pltpu.VMEM((facets, 2, SUB, SUB), BF16),
             pltpu.VMEM((2, (2 * rows - MC) // CELLS, CELLS, 2 * cols), BF16),
             pltpu.VMEM((piece, 2 * cols), F32),
+            pltpu.VMEM((piece // CELLS, CELLS, 2 * cols), F32),
             pair(facets // 2),
             pair(2, 3),
             pair(2, 3),

time: 57.7 us -> 57 us (0.988)
  no operation moved by 1% of the time
where the time goes in v5:
time: 57 us; the launch traced here: 56.2 us
  Pallas kernels  53.5 us (94%)
  local copies, waits for them, and re-layouts  1.49 us (3%)
  between operations  1.29 us (2%)
    pallas_call x1, Pallas kernels, fused(): pl.pallas_call(functools.partial(fused_kernel, facets, pos_v, block), out...  53.5 us
    unnamed x2, local copies, waits for them, and re-layouts  1.49 us

profile of v5, /device:TPU:16, one launch (start us, length us, event | category | flops | bytes accessed | tf_op | source)
XLA Modules:
  0.0 56.2 jit_solution(13783246687122870520)
XLA Ops:
  1.3 53.5 %everything.1 = (f32[1,2,8192]{2,1,0:T(2,128)S(1)}, f32[1,2,176,448]{3,2,1,0:T(8,128)S(1)}) custom-call(f32[2,256,256]{2,1,0:T(8,128)} %constant.4.clone.base, f32[8,2,256]{2,1,0:T(2,128)} %constant.11.turns, s32[32]{0:T(128)} %worker.1, s32[1]{0:T(128)S(6)} %copy.14.count, bf16[1,2,448,704]{3,2,1,0:T(8,128)(2,1)} %bitcast.1, s32[1,2,8192]{2,1,0:T(2,128)} %offsets.1, ...), custom_call_target="tpu_custom_call" | custom-call | tf_op jit(solution)/shard_map/everything/pallas_call | solution.py:962
  54.8 0.6 %copy.12 = f32[1,2,8192]{2,1,0:T(2,128)} copy(f32[1,2,8192]{2,1,0:T(2,128)S(1)} %get-tuple-element.2) | data formatting | bytes 131072
  55.4 0.9 %copy.13 = f32[1,2,176,448]{3,2,1,0:T(8,128)} copy(f32[1,2,176,448]{3,2,1,0:T(8,128)S(1)} %get-tuple-element.3) | data formatting | bytes 1261568
